TPU v7x, 32 devices: a whole 2x2x4 slice. The times are simulated.
32 devices in a mesh: dp: 2 (over core), row: 4 (over y, x), col: 4 (over z).
Axes of the slice: x: 2, y: 2, z: 4, core: 2. Of those that a mesh axis runs over, the one named last changes fastest.
Arguments:
- inputs: bfloat16 [2, 16, 4, 16, 2048], P('dp', 'row', None, None, 'col'), may hold values from -6 to 6
- up_weight: bfloat16 [2048, 4096], P(None, 'col'), may hold values from -0.1875 to 0.1875
- down_weight: bfloat16 [2048, 4096], P(None, 'col'), may hold values from -0.125 to 0.125
- kernel: float32 [125, 4096], P(None, 'col'), may hold values from -0.625 to 0.625
- cotangent: bfloat16 [2, 16, 4, 16, 2048], P('dp', 'row', None, None, 'col'), may hold values from -2 to 2
Outputs:
- block_output: bfloat16 [2, 16, 4, 16, 2048], P('dp', 'row', None, None, 'col')
- input_grad: bfloat16 [2, 16, 4, 16, 2048], P('dp', 'row', None, None, 'col')
- up_grad: bfloat16 [2048, 4096], P(('dp', 'row'), 'col')
- down_grad: bfloat16 [2048, 4096], P(('dp', 'row'), 'col')
- kernel_grad: float32 [125, 4096], P(None, 'col')
All inputs are finite; a program needn't handle non-finite values.
Results may differ from a plain program's by a relative error of at most 0.012.
Values may be sent and summed in bfloat16 or wider, within the bound.
A program may use at most 128 MiB of HBM per device.

v0:
```python
import jax
import jax.numpy as jnp
from jax import lax
from jax.sharding import PartitionSpec as P


def with_halo(shard, sides, width):
    for axis, dim in sides:
        peers, length = (lax.axis_size(axis), shard.shape[dim])
        up = [(i, (i + 1) % peers) for i in range(peers - 1)]
        down = [(j, i) for i, j in up]
        last = lax.slice_in_dim(shard, length - width, length, axis=dim)
        initial = lax.slice_in_dim(shard, 0, width, axis=dim)
        before = lax.ppermute(last, axis, up)
        after = lax.ppermute(initial, axis, down)
        shard = jnp.concatenate([before, shard, after], axis=dim)
    return shard


def depth_margin(field):
    extended = with_halo(field, (("row", 1),), 2)
    return jnp.pad(extended, ((0, 0), (0, 0), (2, 2), (2, 2), (0, 0)))


def stencil_sum(padded, kernel, mirror):
    planes = padded.shape[1] - 4
    tile_x = padded.shape[2] - 4
    tile_y = padded.shape[3] - 4
    result = jnp.zeros(padded.shape[:1] + (planes, tile_x, tile_y, padded.shape[4]), jnp.float32)
    for depth_step in range(5):
        for row_step in range(5):
            for col_step in range(5):
                first_z = depth_step + mirror * (4 - 2 * depth_step)
                first_x = row_step + mirror * (4 - 2 * row_step)
                first_y = col_step + mirror * (4 - 2 * col_step)
                window = padded[
                    :,
                    first_z : first_z + planes,
                    first_x : first_x + tile_x,
                    first_y : first_y + tile_y,
                    :,
                ]
                result = result + kernel[25 * depth_step + 5 * row_step + col_step] * window
    return result


def kernel_terms(padded, grad_field):
    planes = grad_field.shape[1]
    tile_x = grad_field.shape[2]
    tile_y = grad_field.shape[3]
    grad_wide = grad_field.astype(jnp.float32)
    rows_list = []
    for depth_step in range(5):
        for row_step in range(5):
            for col_step in range(5):
                window = padded[
                    :,
                    depth_step : depth_step + planes,
                    row_step : row_step + tile_x,
                    col_step : col_step + tile_y,
                    :,
                ]
                rows_list.append(jnp.sum(window * grad_wide, axis=(0, 1, 2, 3)))
    return jnp.stack(rows_list)


def column_sum(partial_value, field_shape):
    return lax.psum_scatter(
        partial_value.reshape(field_shape).astype(jnp.bfloat16),
        "col",
        scatter_dimension=4,
        tiled=True,
    ).astype(jnp.float32)


def spread_product(left_rows, right_rows):
    return lax.dot_general(
        left_rows, right_rows, (((0,), (0,)), ((), ())), preferred_element_type=jnp.float32
    )


def on_device(inputs, up_weight, down_weight, kernel, cotangent):
    states, planes, tile_x, tile_y, local_width = inputs.shape
    voxels = states * planes * tile_x * tile_y
    local_hidden = up_weight.shape[1]
    contract_last = (((1,), (1,)), ((), ()))
    input_rows, cotangent_rows = (
        lax.all_gather(inputs, "col", axis=4, tiled=True),
        lax.all_gather(cotangent, "col", axis=4, tiled=True),
    )
    full_width = input_rows.shape[4]
    field_shape = (states, planes, tile_x, tile_y, full_width)
    hidden_shape = (states, planes, tile_x, tile_y, local_hidden)
    flat_inputs = input_rows.reshape(voxels, full_width)
    hidden = jnp.dot(flat_inputs, up_weight, preferred_element_type=jnp.float32).astype(
        jnp.bfloat16
    )
    hidden_pad = depth_margin(hidden.reshape(hidden_shape))
    preact = stencil_sum(hidden_pad, kernel, 0)
    activation = jax.nn.silu(preact).astype(jnp.bfloat16)
    flat_act = activation.reshape(voxels, local_hidden)
    mixed_share = column_sum(
        lax.dot_general(flat_act, down_weight, contract_last, preferred_element_type=jnp.float32),
        field_shape,
    )
    block_output = (inputs.astype(jnp.float32) + mixed_share).astype(jnp.bfloat16)
    flat_cotangent = cotangent_rows.reshape(voxels, full_width)
    act_grad = jnp.dot(flat_cotangent, down_weight, preferred_element_type=jnp.float32).reshape(
        hidden_shape
    )
    logistic = jax.nn.sigmoid(preact)
    preact_grad = (act_grad * logistic * (1.0 + preact * (1.0 - logistic))).astype(jnp.bfloat16)
    grad_pad = depth_margin(preact_grad)
    hidden_grad = stencil_sum(grad_pad, kernel, 1).astype(jnp.bfloat16)
    kernel_grad = lax.psum(
        kernel_terms(hidden_pad, preact_grad).astype(jnp.bfloat16), ("dp", "row")
    ).astype(jnp.float32)
    flat_grad_hidden = hidden_grad.reshape(voxels, local_hidden)
    input_share = column_sum(
        lax.dot_general(
            flat_grad_hidden, up_weight, contract_last, preferred_element_type=jnp.float32
        ),
        field_shape,
    )
    input_grad = (cotangent.astype(jnp.float32) + input_share).astype(jnp.bfloat16)
    both_share = lax.psum_scatter(
        jnp.concatenate(
            [
                spread_product(flat_inputs, flat_grad_hidden),
                spread_product(flat_cotangent, flat_act),
            ],
            axis=1,
        ).astype(jnp.bfloat16),
        ("dp", "row"),
        scatter_dimension=0,
        tiled=True,
    ).astype(jnp.float32)
    up_share = both_share[:, :local_hidden]
    down_share = both_share[:, local_hidden:]
    up_grad = up_share.astype(jnp.bfloat16)
    down_grad = down_share.astype(jnp.bfloat16)
    return (block_output, input_grad, up_grad, down_grad, kernel_grad)


def solution(mesh):
    placed = (
        P("dp", "row", None, None, "col"),
        P(None, "col"),
        P(None, "col"),
        P(None, "col"),
        P("dp", "row", None, None, "col"),
    )
    return jax.shard_map(
        on_device,
        mesh=mesh,
        in_specs=placed,
        out_specs=(
            P("dp", "row", None, None, "col"),
            P("dp", "row", None, None, "col"),
            P(("dp", "row"), "col"),
            P(("dp", "row"), "col"),
            P(None, "col"),
        ),
        check_vma=False,
    )
```

profile of v0, /device:TPU:0, one launch (start us, length us, event | category | flops | bytes accessed | tf_op | source)
XLA Modules:
  0.0 385.0 jit_solution(17823461748566457241)
XLA Ops:
  7.9 0.7 all-gather.5.cloned.1.call-update
  8.7 1.3 fusion.328
  10.0 2.0 fusion.327
  12.0 1.9 fusion.326
  13.9 1.9 fusion.325
  15.9 2.0 fusion.324
  17.9 22.3 %all-gather.3.cloned.1.call-done = bf16[1,4,4,16,2048]{4,3,2,1,0:T(8,128)(2,1)} async-done(((bf16[1,4,4,16,512]{4,3,2,1,0:T(8,128)(2,1)}), bf16[1,4,4,16,2048]{4,3,2,1,0:T(8,128)(2,1)}) %all-gather.3.cloned.1.call-update) | async-done | bytes 1048592 | tf_op jit(solution)/shard_map/all_gather | solution.py:88
  40.2 3.8 convolution_convert_fusion
  44.5 1.3 collective-permute-start.1
  45.8 4.7 %collective-permute-start = (bf16[1,2,4,16,1024]{4,3,2,1,0:T(8,128)(2,1)S(1)}, bf16[1,2,4,16,1024]{4,3,2,1,0:T(8,128)(2,1)S(1)}, u32[]{:S(2)}, u32[]{:S(2)}) collective-permute-start(bf16[1,2,4,16,1024]{4,3,2,1,0:T(8,128)(2,1)S(1)} %get-tuple-element.142), channel_id=1, source_target_pairs={{0,4},{4,8},{8,12},{1,5},{5,9},{9,13},{2,6},{6,10},{10,14},{3,7},{... | collective-permute-start | bytes 786440 | tf_op jit(solution)/shard_map/ppermute | solution.py:14
  50.5 1.1 fusion.330
  51.7 1.4 fusion.329
  53.3 2.3 collective-permute-done.1
  55.6 0.8 select_maximum_fusion.2
  57.1 28.9 %fusion.159 = f32[1,4,4,16,1024]{4,3,2,1,0:T(8,128)} fusion(bf16[1,4,4,16,1024]{4,3,2,1,0:T(8,128)(2,1)S(1)} %bitcast.210, f32[1024]{0:T(1024)S(1)} %bitcast.420, f32[1024]{0:T(1024)S(1)} %bitcast.422, f32[1024]{0:T(1024)} %bitcast.366, f32[1024]{0:T(1024)} %bitcast.368, f32[1024]{0:T(1024)} %bitcast.370, f32[1024]{0:T(1024)} %bitcast.372, ...), kind=kLoop, calls=%fused_computation.406 | loop fusion | flops 99090432 | bytes 65523712 | tf_op jit(solution)/shard_map/add | solution.py:43
  86.1 6.9 %fusion.303 = (bf16[1024]{0:T(1024)(128)(2,1)}, bf16[1024]{0:T(1024)(128)(2,1)}, bf16[1024]{0:T(1024)(128)(2,1)}, bf16[1024]{0:T(1024)(128)(2,1)}, bf16[1024]{0:...) fusion(bf16[1,8,8,20,1024]{4,3,2,1,0:T(8,128)(2,1)S(1)} %select, ...), kind=kOutput, calls=%fused_computation.550 | convolution fusion | flops 1086573568 | bytes 13658112 | tf_op jit(solution)/shard_map/dot_general | solution.py:108
  93.1 3.4 fusion.308
  96.5 3.4 fusion.309
  99.9 3.4 fusion.306
  103.3 3.4 fusion.304
  106.7 3.3 fusion.305
  110.0 3.4 fusion.307
  113.8 2.3 fusion.21
  116.0 0.8 stack.622
  121.1 0.7 stack.621
  122.5 0.7 stack.504
  127.2 0.7 stack.528
  129.2 0.7 stack.531
  129.9 0.7 stack.532
  132.6 0.7 stack.536
  135.3 0.7 stack.540
  136.0 0.7 stack.542
  136.7 0.7 stack.543
  138.7 0.7 stack.509
  149.9 0.7 stack.561
  151.9 0.7 stack.564
  153.9 0.7 stack.568
  155.3 0.7 stack.570
  156.6 0.7 stack.572
  157.3 0.7 stack.573
  161.4 0.7 stack.623
  164.0 0.7 stack.600
  165.4 0.7 stack.602
  168.1 0.7 stack.606
  169.4 0.7 stack.608
  173.5 0.7 stack.626
  175.0 10.6 %stack.629 = bf16[125,1024]{1,0:T(8,128)(2,1)} concatenate(bf16[1,1024]{1,0:T(2,128)(2,1)S(1)} %stack.504, bf16[1,1024]{1,0:T(2,128)(2,1)S(1)} %stack.505, bf16[1,1024]{1,0:T(2,128)(2,1)S(1)} %stack.506, bf16[1,1024]{1,0:T(2,128)(2,1)S(1)} %stack.507, bf16[1,1024]{1,0:T(2,128)(2,1)S(1)} %stack.508, bf16[1,1024]{1,0:T(2,128)(2,1)S(1)} %stack.509, bf16[1,1024]{1,0:T(2,128)(2,1)S(1)} %stack.510, ...), dimensions={0} | concatenate | bytes 512000 | tf_op jit(solution)/shard_map/stack | solution.py:64
  185.7 1.3 collective-permute-start.3
  187.0 6.4 %collective-permute-start.2 = (bf16[1,2,4,16,1024]{4,3,2,1,0:T(8,128)(2,1)S(1)}, bf16[1,2,4,16,1024]{4,3,2,1,0:T(8,128)(2,1)S(1)}, u32[]{:S(2)}, u32[]{:S(2)}) collective-permute-start(bf16[1,2,4,16,1024]{4,3,2,1,0:T(8,128)(2,1)S(1)} %get-tuple-element.140), channel_id=1, source_target_pairs={{0,4},{4,8},{8,12},{1,5},{5,9},{9,13},{2,6},{6,10},{10,14},{3,7},{... | collective-permute-start | bytes 786440 | tf_op jit(solution)/shard_map/ppermute | solution.py:14
  193.5 4.5 %fusion.10 = bf16[2048,1024]{0,1:T(8,128)(2,1)} fusion(bf16[1,4,4,16,2048]{4,3,2,1,0:T(8,128)(2,1)} %all-gather.5.cloned.1.call-done, f32[1,4,4,16,1024]{4,3,2,1,0:T(8,128)S(1)} %copy-done.7), kind=kOutput, calls=%fused_computation.143 | convolution fusion | flops 1077149696 | bytes 6291456 | tf_op jit(solution)/shard_map/dot_general | solution.py:77
  198.5 1.1 select_maximum_fusion
  200.0 30.2 %add_convert_fusion = bf16[1,4,4,16,1024]{4,3,2,1,0:T(8,128)(2,1)S(1)} fusion(bf16[1,4,4,16,1024]{4,3,2,1,0:T(8,128)(2,1)S(1)} %copy-done.1, bf16[1,2,4,16,1024]{4,3,2,1,0:T(8,128)(2,1)S(1)} %collective-permute-done.2, bf16[1,2,4,16,1024]{4,3,2,1,0:T(8,128)(2,1)S(1)} %collective-permute-done.3, bf16[1,8,8,20,1024]{4,3,2,1,0:T(8,128)(2,1)S(1)} %select_maximum_fusion, ...), kind=kLoop, calls=%fused_computation.560 | loop fusion | flops 99352576 | bytes 64999424 | tf_op jit(solution)/shard_map/convert_element_type | solution.py:114
  230.2 4.5 %fusion.18 = bf16[1,4,4,16,2048]{4,3,2,1,0:T(8,128)(2,1)} fusion(bf16[2048,1024]{1,0:T(8,128)(2,1)} %param.6, bf16[1,4,4,16,1024]{4,3,2,1,0:T(8,128)(2,1)S(1)} %add_convert_fusion), kind=kOutput, calls=%fused_computation.151 | convolution fusion | flops 1074266112 | bytes 5767168 | tf_op jit(solution)/shard_map/dot_general | solution.py:120
  234.8 4.5 %fusion.9 = bf16[2048,1024]{0,1:T(8,128)(2,1)} fusion(bf16[1,4,4,16,2048]{4,3,2,1,0:T(8,128)(2,1)} %all-gather.3.cloned.1.call-done, bf16[1,4,4,16,1024]{4,3,2,1,0:T(8,128)(2,1)S(1)} %add_convert_fusion), kind=kOutput, calls=%fused_computation.142 | convolution fusion | flops 1075838976 | bytes 5767168 | tf_op jit(solution)/shard_map/dot_general | solution.py:77
  239.3 8.4 %pad_maximum_fusion = bf16[2048,2048]{0,1:T(8,128)(2,1)} fusion(bf16[2048,1024]{0,1:T(8,128)(2,1)} %fusion.10, bf16[2048,1024]{0,1:T(8,128)(2,1)} %fusion.9), kind=kLoop, calls=%fused_computation.130 | loop fusion | flops 16777216 | bytes 16777216 | tf_op jit(solution)/shard_map/concatenate | solution.py:127
  247.7 1.8 convert_element_type.1202
  249.6 23.6 %reduce-scatter.4.cloned.1.call-done = bf16[1,4,4,16,512]{4,3,2,1,0:T(8,128)(2,1)} async-done(((bf16[1,4,4,16,2048]{4,3,2,1,0:T(8,128)(2,1)}), bf16[1,4,4,16,512]{4,3,2,1,0:T(8,128)(2,1)}) %reduce-scatter.4.cloned.1.call-update) | async-done | bytes 262160 | tf_op jit(solution)/shard_map/reduce_scatter | solution.py:68
  273.2 1.7 add_convert_fusion.2
  274.9 26.2 %reduce-scatter.6.cloned.1.call-done = bf16[1,4,4,16,512]{4,3,2,1,0:T(8,128)(2,1)} async-done(((bf16[1,4,4,16,2048]{4,3,2,1,0:T(8,128)(2,1)}), bf16[1,4,4,16,512]{4,3,2,1,0:T(8,128)(2,1)}) %reduce-scatter.6.cloned.1.call-update) | async-done | bytes 262160 | tf_op jit(solution)/shard_map/reduce_scatter | solution.py:68
  301.1 1.7 add_convert_fusion.1
  302.9 71.9 %reduce-scatter.8.cloned.1.call-done = bf16[256,2048]{0,1:T(8,128)(2,1)} async-done(((bf16[2048,2048]{0,1:T(8,128)(2,1)}), bf16[256,2048]{0,1:T(8,128)(2,1)}) %reduce-scatter.8.cloned.1.call-update) | async-done | bytes 1048592 | tf_op jit(solution)/shard_map/reduce_scatter | solution.py:126
  374.8 1.3 fusion.321
  376.1 1.0 copy.11
  377.1 1.0 copy.10
  (433 shorter events, 44.2 us)
Async XLA Ops:
  7.2 33.1 %all-gather.3.cloned.1.call-start = ((), (), s32[]{:S(2)}) async-start(), calls=%async_computation.3 | async-start | bytes 1310720 | tf_op jit(solution)/shard_map/all_gather | solution.py:88
  7.9 78.2 %all-gather.5.cloned.1.call-start = ((), (), s32[]{:S(2)}) async-start(), calls=%async_computation.5 | async-start | bytes 1310720 | tf_op jit(solution)/shard_map/all_gather | solution.py:89
  8.6 239.1 %all-reduce.4.cloned.1.call-start = ((), (), s32[]{:S(2)}) async-start(), calls=%async_computation.8 | async-start | bytes 524288 | tf_op jit(solution)/shard_map/psum | solution.py:115
  44.0 12.7 %copy-start.10 = (f32[1,1024]{1,0:T(1,128)S(1)}, f32[1,1024]{1,0:T(1,128)}, u32[]{:S(2)}) copy-start(f32[1,1024]{1,0:T(1,128)} %get-tuple-element.217) | copy-start | bytes 12292
  44.0 12.7 %copy-start.12 = (f32[1,1024]{1,0:T(1,128)S(1)}, f32[1,1024]{1,0:T(1,128)}, u32[]{:S(2)}) copy-start(f32[1,1024]{1,0:T(1,128)} %get-tuple-element.218) | copy-start | bytes 12292
  44.0 12.7 %copy-start.14 = (f32[1,1024]{1,0:T(1,128)S(1)}, f32[1,1024]{1,0:T(1,128)}, u32[]{:S(2)}) copy-start(f32[1,1024]{1,0:T(1,128)} %get-tuple-element.181) | copy-start | bytes 12292
  44.0 12.7 %copy-start.16 = (f32[1,1024]{1,0:T(1,128)S(1)}, f32[1,1024]{1,0:T(1,128)}, u32[]{:S(2)}) copy-start(f32[1,1024]{1,0:T(1,128)} %get-tuple-element.182) | copy-start | bytes 12292
  44.1 12.7 %copy-start.18 = (f32[1,1024]{1,0:T(1,128)S(1)}, f32[1,1024]{1,0:T(1,128)}, u32[]{:S(2)}) copy-start(f32[1,1024]{1,0:T(1,128)} %get-tuple-element.183) | copy-start | bytes 12292
  44.1 12.7 %copy-start.20 = (f32[1,1024]{1,0:T(1,128)S(1)}, f32[1,1024]{1,0:T(1,128)}, u32[]{:S(2)}) copy-start(f32[1,1024]{1,0:T(1,128)} %get-tuple-element.184) | copy-start | bytes 12292
  44.1 12.7 %copy-start.22 = (f32[1,1024]{1,0:T(1,128)S(1)}, f32[1,1024]{1,0:T(1,128)}, u32[]{:S(2)}) copy-start(f32[1,1024]{1,0:T(1,128)} %get-tuple-element.185) | copy-start | bytes 12292
  44.1 12.7 %copy-start.24 = (f32[1,1024]{1,0:T(1,128)S(1)}, f32[1,1024]{1,0:T(1,128)}, u32[]{:S(2)}) copy-start(f32[1,1024]{1,0:T(1,128)} %get-tuple-element.186) | copy-start | bytes 12292
  44.1 12.7 %copy-start.26 = (f32[1,1024]{1,0:T(1,128)S(1)}, f32[1,1024]{1,0:T(1,128)}, u32[]{:S(2)}) copy-start(f32[1,1024]{1,0:T(1,128)} %get-tuple-element.187) | copy-start | bytes 12292
  44.1 12.7 %copy-start.28 = (f32[1,1024]{1,0:T(1,128)S(1)}, f32[1,1024]{1,0:T(1,128)}, u32[]{:S(2)}) copy-start(f32[1,1024]{1,0:T(1,128)} %get-tuple-element.188) | copy-start | bytes 12292
  44.1 12.7 %copy-start.30 = (f32[1,1024]{1,0:T(1,128)S(1)}, f32[1,1024]{1,0:T(1,128)}, u32[]{:S(2)}) copy-start(f32[1,1024]{1,0:T(1,128)} %get-tuple-element.189) | copy-start | bytes 12292
  44.1 12.7 %copy-start.32 = (f32[1,1024]{1,0:T(1,128)S(1)}, f32[1,1024]{1,0:T(1,128)}, u32[]{:S(2)}) copy-start(f32[1,1024]{1,0:T(1,128)} %get-tuple-element.190) | copy-start | bytes 12292
  44.1 12.7 %copy-start.34 = (f32[1,1024]{1,0:T(1,128)S(1)}, f32[1,1024]{1,0:T(1,128)}, u32[]{:S(2)}) copy-start(f32[1,1024]{1,0:T(1,128)} %get-tuple-element.191) | copy-start | bytes 12292
  44.1 12.7 %copy-start.36 = (f32[1,1024]{1,0:T(1,128)S(1)}, f32[1,1024]{1,0:T(1,128)}, u32[]{:S(2)}) copy-start(f32[1,1024]{1,0:T(1,128)} %get-tuple-element.192) | copy-start | bytes 12292
  44.2 12.7 %copy-start.38 = (f32[1,1024]{1,0:T(1,128)S(1)}, f32[1,1024]{1,0:T(1,128)}, u32[]{:S(2)}) copy-start(f32[1,1024]{1,0:T(1,128)} %get-tuple-element.193) | copy-start | bytes 12292
  44.5 11.1 %collective-permute-start.1 = (bf16[1,2,4,16,1024]{4,3,2,1,0:T(8,128)(2,1)S(1)}, bf16[1,2,4,16,1024]{4,3,2,1,0:T(8,128)(2,1)S(1)}, u32[]{:S(2)}, u32[]{:S(2)}) collective-permute-start(bf16[1,2,4,16,1024]{4,3,2,1,0:T(8,128)(2,1)S(1)} %get-tuple-element.141), channel_id=1, source_target_pairs={{4,0},{8,4},{12,8},{5,1},{9,5},{13,9},{6,2},{10,6},{14,10},{7,3},{... | collective-permute-start | bytes 786440 | tf_op jit(solution)/shard_map/ppermute | solution.py:15
  45.8 9.8 %collective-permute-start = (bf16[1,2,4,16,1024]{4,3,2,1,0:T(8,128)(2,1)S(1)}, bf16[1,2,4,16,1024]{4,3,2,1,0:T(8,128)(2,1)S(1)}, u32[]{:S(2)}, u32[]{:S(2)}) collective-permute-start(bf16[1,2,4,16,1024]{4,3,2,1,0:T(8,128)(2,1)S(1)} %get-tuple-element.142), channel_id=1, source_target_pairs={{0,4},{4,8},{8,12},{1,5},{5,9},{9,13},{2,6},{6,10},{10,14},{3,7},{... | collective-permute-start | bytes 786440 | tf_op jit(solution)/shard_map/ppermute | solution.py:14
  93.1 16.9 %copy-start = (bf16[1,4,4,16,1024]{4,3,2,1,0:T(8,128)(2,1)}, bf16[1,4,4,16,1024]{4,3,2,1,0:T(8,128)(2,1)S(1)}, u32[]{:S(2)}) copy-start(bf16[1,4,4,16,1024]{4,3,2,1,0:T(8,128)(2,1)S(1)} %get-tuple-element.268) | copy-start | bytes 1572868
  113.4 60.1 %copy-start.154 = (bf16[1024]{0:T(1024)(128)(2,1)S(1)}, bf16[1024]{0:T(1024)(128)(2,1)}, u32[]{:S(2)}) copy-start(bf16[1024]{0:T(1024)(128)(2,1)} %get-tuple-element.82) | copy-start | bytes 6148
  113.4 60.8 %copy-start.153 = (bf16[1024]{0:T(1024)(128)(2,1)S(1)}, bf16[1024]{0:T(1024)(128)(2,1)}, u32[]{:S(2)}) copy-start(bf16[1024]{0:T(1024)(128)(2,1)} %get-tuple-element.83) | copy-start | bytes 6148
  113.4 60.8 %copy-start.152 = (bf16[1024]{0:T(1024)(128)(2,1)S(1)}, bf16[1024]{0:T(1024)(128)(2,1)}, u32[]{:S(2)}) copy-start(bf16[1024]{0:T(1024)(128)(2,1)} %get-tuple-element.84) | copy-start | bytes 6148
  113.4 60.8 %copy-start.151 = (bf16[1024]{0:T(1024)(128)(2,1)S(1)}, bf16[1024]{0:T(1024)(128)(2,1)}, u32[]{:S(2)}) copy-start(bf16[1024]{0:T(1024)(128)(2,1)} %get-tuple-element.85) | copy-start | bytes 6148
  113.5 60.8 %copy-start.150 = (bf16[1024]{0:T(1024)(128)(2,1)S(1)}, bf16[1024]{0:T(1024)(128)(2,1)}, u32[]{:S(2)}) copy-start(bf16[1024]{0:T(1024)(128)(2,1)} %get-tuple-element.86) | copy-start | bytes 6148
  113.5 60.8 %copy-start.149 = (bf16[1024]{0:T(1024)(128)(2,1)S(1)}, bf16[1024]{0:T(1024)(128)(2,1)}, u32[]{:S(2)}) copy-start(bf16[1024]{0:T(1024)(128)(2,1)} %get-tuple-element.87) | copy-start | bytes 6148
  113.5 60.8 %copy-start.148 = (bf16[1024]{0:T(1024)(128)(2,1)S(1)}, bf16[1024]{0:T(1024)(128)(2,1)}, u32[]{:S(2)}) copy-start(bf16[1024]{0:T(1024)(128)(2,1)} %get-tuple-element.88) | copy-start | bytes 6148
  113.5 60.9 %copy-start.147 = (bf16[1024]{0:T(1024)(128)(2,1)S(1)}, bf16[1024]{0:T(1024)(128)(2,1)}, u32[]{:S(2)}) copy-start(bf16[1024]{0:T(1024)(128)(2,1)} %get-tuple-element.89) | copy-start | bytes 6148
  113.5 60.9 %copy-start.146 = (bf16[1024]{0:T(1024)(128)(2,1)S(1)}, bf16[1024]{0:T(1024)(128)(2,1)}, u32[]{:S(2)}) copy-start(bf16[1024]{0:T(1024)(128)(2,1)} %get-tuple-element.90) | copy-start | bytes 6148
  113.5 60.9 %copy-start.145 = (bf16[1024]{0:T(1024)(128)(2,1)S(1)}, bf16[1024]{0:T(1024)(128)(2,1)}, u32[]{:S(2)}) copy-start(bf16[1024]{0:T(1024)(128)(2,1)} %get-tuple-element.91) | copy-start | bytes 6148
  113.5 60.9 %copy-start.144 = (bf16[1024]{0:T(1024)(128)(2,1)S(1)}, bf16[1024]{0:T(1024)(128)(2,1)}, u32[]{:S(2)}) copy-start(bf16[1024]{0:T(1024)(128)(2,1)} %get-tuple-element.92) | copy-start | bytes 6148
  113.5 60.9 %copy-start.143 = (bf16[1024]{0:T(1024)(128)(2,1)S(1)}, bf16[1024]{0:T(1024)(128)(2,1)}, u32[]{:S(2)}) copy-start(bf16[1024]{0:T(1024)(128)(2,1)} %get-tuple-element.93) | copy-start | bytes 6148
  113.5 60.9 %copy-start.142 = (bf16[1024]{0:T(1024)(128)(2,1)S(1)}, bf16[1024]{0:T(1024)(128)(2,1)}, u32[]{:S(2)}) copy-start(bf16[1024]{0:T(1024)(128)(2,1)} %get-tuple-element.94) | copy-start | bytes 6148
  113.5 60.9 %copy-start.141 = (bf16[1024]{0:T(1024)(128)(2,1)S(1)}, bf16[1024]{0:T(1024)(128)(2,1)}, u32[]{:S(2)}) copy-start(bf16[1024]{0:T(1024)(128)(2,1)} %get-tuple-element.95) | copy-start | bytes 6148
  113.5 60.9 %copy-start.140 = (bf16[1024]{0:T(1024)(128)(2,1)S(1)}, bf16[1024]{0:T(1024)(128)(2,1)}, u32[]{:S(2)}) copy-start(bf16[1024]{0:T(1024)(128)(2,1)} %get-tuple-element.96) | copy-start | bytes 6148
  113.6 61.0 %copy-start.139 = (bf16[1024]{0:T(1024)(128)(2,1)S(1)}, bf16[1024]{0:T(1024)(128)(2,1)}, u32[]{:S(2)}) copy-start(bf16[1024]{0:T(1024)(128)(2,1)} %get-tuple-element.97) | copy-start | bytes 6148
  113.6 61.0 %copy-start.138 = (bf16[1024]{0:T(1024)(128)(2,1)S(1)}, bf16[1024]{0:T(1024)(128)(2,1)}, u32[]{:S(2)}) copy-start(bf16[1024]{0:T(1024)(128)(2,1)} %get-tuple-element.98) | copy-start | bytes 6148
  113.6 61.0 %copy-start.136 = (bf16[1024]{0:T(1024)(128)(2,1)S(1)}, bf16[1024]{0:T(1024)(128)(2,1)}, u32[]{:S(2)}) copy-start(bf16[1024]{0:T(1024)(128)(2,1)} %get-tuple-element.99) | copy-start | bytes 6148
  113.6 61.0 %copy-start.137 = (bf16[1024]{0:T(1024)(128)(2,1)S(1)}, bf16[1024]{0:T(1024)(128)(2,1)}, u32[]{:S(2)}) copy-start(bf16[1024]{0:T(1024)(128)(2,1)} %get-tuple-element.47) | copy-start | bytes 6148
  113.6 61.0 %copy-start.135 = (bf16[1024]{0:T(1024)(128)(2,1)S(1)}, bf16[1024]{0:T(1024)(128)(2,1)}, u32[]{:S(2)}) copy-start(bf16[1024]{0:T(1024)(128)(2,1)} %get-tuple-element.48) | copy-start | bytes 6148
  113.6 61.0 %copy-start.134 = (bf16[1024]{0:T(1024)(128)(2,1)S(1)}, bf16[1024]{0:T(1024)(128)(2,1)}, u32[]{:S(2)}) copy-start(bf16[1024]{0:T(1024)(128)(2,1)} %get-tuple-element.49) | copy-start | bytes 6148
  113.6 61.0 %copy-start.133 = (bf16[1024]{0:T(1024)(128)(2,1)S(1)}, bf16[1024]{0:T(1024)(128)(2,1)}, u32[]{:S(2)}) copy-start(bf16[1024]{0:T(1024)(128)(2,1)} %get-tuple-element.50) | copy-start | bytes 6148
  113.6 61.0 %copy-start.132 = (bf16[1024]{0:T(1024)(128)(2,1)S(1)}, bf16[1024]{0:T(1024)(128)(2,1)}, u32[]{:S(2)}) copy-start(bf16[1024]{0:T(1024)(128)(2,1)} %get-tuple-element.51) | copy-start | bytes 6148
  113.6 61.1 %copy-start.131 = (bf16[1024]{0:T(1024)(128)(2,1)S(1)}, bf16[1024]{0:T(1024)(128)(2,1)}, u32[]{:S(2)}) copy-start(bf16[1024]{0:T(1024)(128)(2,1)} %get-tuple-element.52) | copy-start | bytes 6148
  113.7 61.1 %copy-start.130 = (bf16[1024]{0:T(1024)(128)(2,1)S(1)}, bf16[1024]{0:T(1024)(128)(2,1)}, u32[]{:S(2)}) copy-start(bf16[1024]{0:T(1024)(128)(2,1)} %get-tuple-element.53) | copy-start | bytes 6148
  113.7 61.1 %copy-start.129 = (bf16[1024]{0:T(1024)(128)(2,1)S(1)}, bf16[1024]{0:T(1024)(128)(2,1)}, u32[]{:S(2)}) copy-start(bf16[1024]{0:T(1024)(128)(2,1)} %get-tuple-element.54) | copy-start | bytes 6148
  113.7 61.1 %copy-start.128 = (bf16[1024]{0:T(1024)(128)(2,1)S(1)}, bf16[1024]{0:T(1024)(128)(2,1)}, u32[]{:S(2)}) copy-start(bf16[1024]{0:T(1024)(128)(2,1)} %get-tuple-element.55) | copy-start | bytes 6148
  113.7 61.1 %copy-start.127 = (bf16[1024]{0:T(1024)(128)(2,1)S(1)}, bf16[1024]{0:T(1024)(128)(2,1)}, u32[]{:S(2)}) copy-start(bf16[1024]{0:T(1024)(128)(2,1)} %get-tuple-element.56) | copy-start | bytes 6148
  113.7 61.1 %copy-start.126 = (bf16[1024]{0:T(1024)(128)(2,1)S(1)}, bf16[1024]{0:T(1024)(128)(2,1)}, u32[]{:S(2)}) copy-start(bf16[1024]{0:T(1024)(128)(2,1)} %get-tuple-element.57) | copy-start | bytes 6148
  113.7 61.1 %copy-start.125 = (bf16[1024]{0:T(1024)(128)(2,1)S(1)}, bf16[1024]{0:T(1024)(128)(2,1)}, u32[]{:S(2)}) copy-start(bf16[1024]{0:T(1024)(128)(2,1)} %get-tuple-element.58) | copy-start | bytes 6148
  113.7 61.2 %copy-start.124 = (bf16[1024]{0:T(1024)(128)(2,1)S(1)}, bf16[1024]{0:T(1024)(128)(2,1)}, u32[]{:S(2)}) copy-start(bf16[1024]{0:T(1024)(128)(2,1)} %get-tuple-element.59) | copy-start | bytes 6148
  113.7 61.2 %copy-start.123 = (bf16[1024]{0:T(1024)(128)(2,1)S(1)}, bf16[1024]{0:T(1024)(128)(2,1)}, u32[]{:S(2)}) copy-start(bf16[1024]{0:T(1024)(128)(2,1)} %get-tuple-element.60) | copy-start | bytes 6148
  113.7 61.2 %copy-start.122 = (bf16[1024]{0:T(1024)(128)(2,1)S(1)}, bf16[1024]{0:T(1024)(128)(2,1)}, u32[]{:S(2)}) copy-start(bf16[1024]{0:T(1024)(128)(2,1)} %get-tuple-element.61) | copy-start | bytes 6148
  113.7 61.2 %copy-start.121 = (bf16[1024]{0:T(1024)(128)(2,1)S(1)}, bf16[1024]{0:T(1024)(128)(2,1)}, u32[]{:S(2)}) copy-start(bf16[1024]{0:T(1024)(128)(2,1)} %get-tuple-element.62) | copy-start | bytes 6148
  113.8 61.2 %copy-start.120 = (bf16[1024]{0:T(1024)(128)(2,1)S(1)}, bf16[1024]{0:T(1024)(128)(2,1)}, u32[]{:S(2)}) copy-start(bf16[1024]{0:T(1024)(128)(2,1)} %get-tuple-element.63) | copy-start | bytes 6148
  116.0 77.5 %copy-start.7 = (f32[1,4,4,16,1024]{4,3,2,1,0:T(8,128)S(1)}, f32[1,4,4,16,1024]{4,3,2,1,0:T(8,128)}, u32[]{:S(2)}) copy-start(f32[1,4,4,16,1024]{4,3,2,1,0:T(8,128)} %fusion.159) | copy-start | bytes 3145732
  185.6 87.5 %reduce-scatter.4.cloned.1.call-start = ((), (), s32[]{:S(2)}) async-start(), calls=%async_computation.4 | async-start | bytes 1310720 | tf_op jit(solution)/shard_map/reduce_scatter | solution.py:68
  185.7 12.7 %collective-permute-start.3 = (bf16[1,2,4,16,1024]{4,3,2,1,0:T(8,128)(2,1)S(1)}, bf16[1,2,4,16,1024]{4,3,2,1,0:T(8,128)(2,1)S(1)}, u32[]{:S(2)}, u32[]{:S(2)}) collective-permute-start(bf16[1,2,4,16,1024]{4,3,2,1,0:T(8,128)(2,1)S(1)} %get-tuple-element.139), channel_id=1, source_target_pairs={{4,0},{8,4},{12,8},{5,1},{9,5},{13,9},{6,2},{10,6},{14,10},{7,3},{... | collective-permute-start | bytes 786440 | tf_op jit(solution)/shard_map/ppermute | solution.py:15
  187.0 11.4 %collective-permute-start.2 = (bf16[1,2,4,16,1024]{4,3,2,1,0:T(8,128)(2,1)S(1)}, bf16[1,2,4,16,1024]{4,3,2,1,0:T(8,128)(2,1)S(1)}, u32[]{:S(2)}, u32[]{:S(2)}) collective-permute-start(bf16[1,2,4,16,1024]{4,3,2,1,0:T(8,128)(2,1)S(1)} %get-tuple-element.140), channel_id=1, source_target_pairs={{0,4},{4,8},{8,12},{1,5},{5,9},{9,13},{2,6},{6,10},{10,14},{3,7},{... | collective-permute-start | bytes 786440 | tf_op jit(solution)/shard_map/ppermute | solution.py:14
  193.5 107.7 %reduce-scatter.6.cloned.1.call-start = ((), (), s32[]{:S(2)}) async-start(), calls=%async_computation.6 | async-start | bytes 1310720 | tf_op jit(solution)/shard_map/reduce_scatter | solution.py:68
  234.8 140.0 %reduce-scatter.8.cloned.1.call-start = ((), (), s32[]{:S(2)}) async-start(), calls=%async_computation.7 | async-start | bytes 9437184 | tf_op jit(solution)/shard_map/reduce_scatter | solution.py:126
  247.7 25.5 %copy-start.8 = (bf16[1,4,4,16,512]{4,3,2,1,0:T(8,128)(2,1)S(1)}, bf16[1,4,4,16,512]{4,3,2,1,0:T(8,128)(2,1)}, u32[]{:S(2)}) copy-start(bf16[1,4,4,16,512]{4,3,2,1,0:T(8,128)(2,1)} %param.5) | copy-start | bytes 786436
  247.7 53.5 %copy-start.9 = (bf16[1,4,4,16,512]{4,3,2,1,0:T(8,128)(2,1)S(1)}, bf16[1,4,4,16,512]{4,3,2,1,0:T(8,128)(2,1)}, u32[]{:S(2)}) copy-start(bf16[1,4,4,16,512]{4,3,2,1,0:T(8,128)(2,1)} %param.9) | copy-start | bytes 786436
  (102 other events, 529.4 us)
Sparse Core Ops, SparseCore 0:
  9.6 30.6 all-gather.2
  41.8 27.4 all-gather.4
  185.8 58.5 all-reduce.3
  246.6 26.5 reduce-scatter.3
  275.3 25.7 reduce-scatter.5
  304.9 69.9 reduce-scatter.7
where the time goes:
time: 388 us; the launch traced here: 385 us
  waiting for transfers between devices  148 us (38%)
  other arithmetic  95.6 us (25%)
  local copies, waits for them, and re-layouts  84.1 us (22%)
  matrix products  26.5 us (7%)
  between operations  16.9 us (4%)
  starting transfers between devices  14 us (4%)
    reduce_scatter x1, waiting for transfers between devices, on_device(): lax.psum_scatter(jnp.concatenate([spread_product(flat_inputs, flat_grad_h...  71.9 us
    another operation x126, local copies, waits for them, and re-layouts, kernel_terms(): return jnp.stack(rows_list)  68.4 us
    reduce_scatter x2, waiting for transfers between devices, column_sum(): lax.psum_scatter(partial_value.reshape(field_shape).astype(jnp.bfloat16),...  49.8 us
    convert_element_type x1, other arithmetic, on_device(): hidden_grad = stencil_sum(grad_pad, kernel, 1).astype(jnp.bfloat16)  30.2 us
    add x1, other arithmetic, stencil_sum(): result = result + kernel[25 * depth_step + 5 * row_step + col_step] * window  28.9 us
    all_gather x1, waiting for transfers between devices, on_device(): lax.all_gather(inputs, 'col', axis=4, tiled=True)  22.3 us
    reduce_sum x7, other arithmetic, kernel_terms(): rows_list.append(jnp.sum(window * grad_wide, axis=(0, 1, 2, 3)))  20.7 us
    slice x7, local copies, waits for them, and re-layouts, stencil_sum(): result = result + kernel[25 * depth_step + 5 * row_step + col_step] * window  11.7 us
  transfers between devices with their start and end apart: 10, of which 5 were waited for; matrix products, arithmetic and copies ran while one was open for 27% of the time, Pallas kernels for 0%

commit v1 on v0

--- a/solution.py
+++ b/solution.py
@@ -2,6 +2,18 @@
 import jax.numpy as jnp
 from jax import lax
 from jax.sharding import PartitionSpec as P
+
+
+def gather_by_bits(x, axis, dim):
+    ways, here = (lax.axis_size(axis), lax.axis_index(axis))
+    grown, reach = (x, 1)
+    while reach < ways:
+        theirs = lax.ppermute(grown, axis, [(d, d ^ reach) for d in range(ways)])
+        mine_first = jnp.concatenate([grown, theirs], axis=dim)
+        theirs_first = jnp.concatenate([theirs, grown], axis=dim)
+        grown = jnp.where(here & reach == 0, mine_first, theirs_first)
+        reach = 2 * reach
+    return grown
 
 
 def with_halo(shard, sides, width):
@@ -85,7 +97,7 @@
     local_hidden = up_weight.shape[1]
     contract_last = (((1,), (1,)), ((), ()))
     input_rows, cotangent_rows = (
-        lax.all_gather(inputs, "col", axis=4, tiled=True),
+        gather_by_bits(inputs, "col", 4),
         lax.all_gather(cotangent, "col", axis=4, tiled=True),
     )
     full_width = input_rows.shape[4]

time: 388 us -> 345 us (0.89)
  local copies, waits for them, and re-layouts: 84.1 us -> 27.4 us
  waiting for transfers between devices: 148 us -> 157 us
  starting transfers between devices: 14 us -> 19.9 us
    another operation x126, local copies, waits for them, and re-layouts: 68.4 us -> 11.3 us  [kernel_terms(): return jnp.stack(rows_list)]
    ppermute x0 -> x2, waiting for transfers between devices: none -> 34.4 us  [gather_by_bits(): theirs = lax.ppermute(grown, axis, [(d, d ^ reach) for d in range(ways)])]
    all_gather x1 -> x0, waiting for transfers between devices: 22.3 us -> none  [on_device(): lax.all_gather(inputs, 'col', axis=4, tiled=True)]
    ppermute x0 -> x2, starting transfers between devices: none -> 5.74 us  [gather_by_bits(): theirs = lax.ppermute(grown, axis, [(d, d ^ reach) for d in range(ways)])]
  transfers between devices with their start and end apart: 10 -> 11, of which waited for: 5 -> 5; matrix products, arithmetic and copies ran while one was open for 27% -> 33% of each run, Pallas kernels for 0% -> 0%
where the time goes in v1:
time: 345 us; the launch traced here: 344 us
  waiting for transfers between devices  157 us (46%)
  other arithmetic  96.2 us (28%)
  local copies, waits for them, and re-layouts  27.4 us (8%)
  matrix products  26.9 us (8%)
  starting transfers between devices  19.9 us (6%)
  between operations  16.6 us (5%)
    reduce_scatter x1, waiting for transfers between devices, on_device(): lax.psum_scatter(jnp.concatenate([spread_product(flat_inputs, flat_grad_h...  71.9 us
    reduce_scatter x2, waiting for transfers between devices, column_sum(): lax.psum_scatter(partial_value.reshape(field_shape).astype(jnp.bfloat16),...  47.3 us
    ppermute x2, waiting for transfers between devices, gather_by_bits(): theirs = lax.ppermute(grown, axis, [(d, d ^ reach) for d in range(ways)])  34.4 us
    convert_element_type x1, other arithmetic, on_device(): hidden_grad = stencil_sum(grad_pad, kernel, 1).astype(jnp.bfloat16)  30.2 us
    add x1, other arithmetic, stencil_sum(): result = result + kernel[25 * depth_step + 5 * row_step + col_step] * window  29.6 us
    reduce_sum x7, other arithmetic, kernel_terms(): rows_list.append(jnp.sum(window * grad_wide, axis=(0, 1, 2, 3)))  17.2 us
    slice x7, local copies, waits for them, and re-layouts, stencil_sum(): result = result + kernel[25 * depth_step + 5 * row_step + col_step] * window  12.3 us
    another operation x126, local copies, waits for them, and re-layouts, kernel_terms(): return jnp.stack(rows_list)  11.3 us
  transfers between devices with their start and end apart: 11, of which 5 were waited for; matrix products, arithmetic and copies ran while one was open for 33% of the time, Pallas kernels for 0%

profile of v1, /device:TPU:0, one launch (start us, length us, event | category | flops | bytes accessed | tf_op | source)
XLA Modules:
  0.0 343.7 jit_solution(17093727181631470255)
XLA Ops:
  7.2 0.0 all-gather.2.cloned.1.call-start
  7.2 0.7 all-gather.2.cloned.1.call-update
  7.9 0.0 all-reduce.4.cloned.1.call-start
  7.9 3.1 collective-permute-start
  11.0 1.3 fusion.340
  12.3 2.0 fusion.339
  14.3 1.9 fusion.338
  16.3 1.3 fusion.337
  17.8 1.3 maximum_select_fusion.5
  19.1 2.7 collective-permute-start.1
  21.7 2.0 fusion.336
  23.9 2.0 fusion.341
  25.9 1.2 maximum_select_fusion.4
  27.2 34.4 %collective-permute-done.1 = bf16[1,4,4,16,1024]{4,3,2,1,0:T(8,128)(2,1)S(1)} collective-permute-done((bf16[1,4,4,16,1024]{4,3,2,1,0:T(8,128)(2,1)S(1)}, bf16[1,4,4,16,1024]{4,3,2,1,0:T(8,128)(2,1)S(1)}, u32[]{:S(2)}, u32[]{:S(2)}) %collective-permute-start.1) | collective-permute-done | bytes 524320 | tf_op jit(solution)/shard_map/ppermute | solution.py:11
  61.5 3.7 %convolution_convert_fusion = bf16[256,1024]{1,0:T(8,128)(2,1)S(1)} fusion(bf16[2048,1024]{1,0:T(8,128)(2,1)} %param.6, bf16[256,1024]{1,0:T(8,128)(2,1)S(1)} %bitcast.399, bf16[256,1024]{1,0:T(8,128)(2,1)S(1)} %maximum_select_fusion.4, pred[]{:T(512)S(6)} %eq.6), kind=kOutput, calls=%fused_computation.281 | convolution fusion | flops 1078722560 | bytes 5767169 | tf_op jit(solution)/shard_map/dot_general | solution.py:107
  65.2 0.0 copy-start.2
  65.5 1.4 collective-permute-start.3
  66.9 4.7 %collective-permute-start.2 = (bf16[1,2,4,16,1024]{4,3,2,1,0:T(8,128)(2,1)S(1)}, bf16[1,2,4,16,1024]{4,3,2,1,0:T(8,128)(2,1)S(1)}, u32[]{:S(2)}, u32[]{:S(2)}) collective-permute-start(bf16[1,2,4,16,1024]{4,3,2,1,0:T(8,128)(2,1)S(1)} %get-tuple-element.142), channel_id=1, source_target_pairs={{0,4},{4,8},{8,12},{1,5},{5,9},{9,13},{2,6},{6,10},{10,14},{3,7},{... | collective-permute-start | bytes 786440 | tf_op jit(solution)/shard_map/ppermute | solution.py:26
  71.7 1.7 fusion.342
  73.4 1.0 maximum_select_fusion.6
  74.4 2.4 collective-permute-done.3
  76.7 0.9 select_maximum_fusion.2
  78.2 29.6 %fusion.158 = f32[1,4,4,16,1024]{4,3,2,1,0:T(8,128)} fusion(bf16[1,4,4,16,1024]{4,3,2,1,0:T(8,128)(2,1)S(1)} %bitcast.207, f32[1024]{0:T(1024)} %bitcast.128, f32[1024]{0:T(1024)} %bitcast.127, f32[1024]{0:T(1024)S(1)} %bitcast.367, f32[1024]{0:T(1024)S(1)} %bitcast.369, f32[1024]{0:T(1024)S(1)} %bitcast.371, f32[1024]{0:T(1024)S(1)} %bitcast.373, ...), kind=kLoop, calls=%fused_computation.405 | loop fusion | flops 99090432 | bytes 65523712 | tf_op jit(solution)/shard_map/add | solution.py:55
  107.8 0.0 all-gather.2.cloned.1.call-done
  107.8 6.3 %fusion.302 = (bf16[1024]{0:T(1024)(128)(2,1)S(1)}, bf16[1024]{0:T(1024)(128)(2,1)S(1)}, bf16[1024]{0:T(1024)(128)(2,1)S(1)}, bf16[1024]{0:T(1024)(128)(2,1)S(1)...) fusion(bf16[1,8,8,20,1024]{4,3,2,1,0:T(8,128)(2,1)S(1)} %select, ...), kind=kOutput, calls=%fused_computation.549 | convolution fusion | flops 1086573568 | bytes 13658112 | tf_op jit(solution)/shard_map/dot_general | solution.py:120
  114.2 0.0 copy-start
  114.2 2.8 fusion.307
  117.0 2.8 fusion.308
  119.8 3.0 fusion.305
  122.8 2.8 fusion.303
  125.6 2.6 fusion.304
  128.2 0.0 copy-start.3
  128.2 0.0 copy-start.6
  128.2 0.0 copy-start.8
  128.3 2.8 fusion.306
  131.1 0.4 fusion.296
  133.2 10.6 %stack.629 = bf16[125,1024]{1,0:T(8,128)(2,1)} concatenate(bf16[1,1024]{1,0:T(2,128)(2,1)S(1)} %stack.504, bf16[1,1024]{1,0:T(2,128)(2,1)S(1)} %stack.505, bf16[1,1024]{1,0:T(2,128)(2,1)S(1)} %stack.506, bf16[1,1024]{1,0:T(2,128)(2,1)S(1)} %stack.507, bf16[1,1024]{1,0:T(2,128)(2,1)S(1)} %stack.508, bf16[1,1024]{1,0:T(2,128)(2,1)S(1)} %stack.509, bf16[1,1024]{1,0:T(2,128)(2,1)S(1)} %stack.510, ...), dimensions={0} | concatenate | bytes 512000 | tf_op jit(solution)/shard_map/stack | solution.py:76
  143.8 0.0 all-reduce.4.cloned.1.call-update
  143.8 0.0 reduce-scatter.4.cloned.1.call-start
  143.9 1.3 collective-permute-start.5
  145.2 0.0 copy-start.1
  145.2 6.5 %collective-permute-start.4 = (bf16[1,2,4,16,1024]{4,3,2,1,0:T(8,128)(2,1)S(1)}, bf16[1,2,4,16,1024]{4,3,2,1,0:T(8,128)(2,1)S(1)}, u32[]{:S(2)}, u32[]{:S(2)}) collective-permute-start(bf16[1,2,4,16,1024]{4,3,2,1,0:T(8,128)(2,1)S(1)} %get-tuple-element.140), channel_id=1, source_target_pairs={{0,4},{4,8},{8,12},{1,5},{5,9},{9,13},{2,6},{6,10},{10,14},{3,7},{... | collective-permute-start | bytes 786440 | tf_op jit(solution)/shard_map/ppermute | solution.py:26
  151.7 4.5 %fusion.20 = bf16[1,4,4,16,2048]{4,3,2,1,0:T(8,128)(2,1)} fusion(bf16[2048,1024]{1,0:T(8,128)(2,1)} %param.7, f32[1,4,4,16,1024]{4,3,2,1,0:T(8,128)S(1)} %copy-done.9), kind=kOutput, calls=%fused_computation.151 | convolution fusion | flops 1075576832 | bytes 6291456 | tf_op jit(solution)/shard_map/dot_general | solution.py:115
  156.5 0.0 reduce-scatter.4.cloned.1.call-update
  156.5 0.0 reduce-scatter.6.cloned.1.call-start
  156.6 1.1 select_maximum_fusion
  158.1 30.2 %add_convert_fusion = bf16[1,4,4,16,1024]{4,3,2,1,0:T(8,128)(2,1)S(1)} fusion(bf16[1,4,4,16,1024]{4,3,2,1,0:T(8,128)(2,1)S(1)} %copy-done.1, bf16[1,2,4,16,1024]{4,3,2,1,0:T(8,128)(2,1)S(1)} %collective-permute-done.4, bf16[1,2,4,16,1024]{4,3,2,1,0:T(8,128)(2,1)S(1)} %collective-permute-done.5, bf16[1,8,8,20,1024]{4,3,2,1,0:T(8,128)(2,1)S(1)} %select_maximum_fusion, ...), kind=kLoop, calls=%fused_computation.570 | loop fusion | flops 99352576 | bytes 64999424 | tf_op jit(solution)/shard_map/convert_element_type | solution.py:126
  188.4 4.5 %fusion.17 = bf16[1,4,4,16,2048]{4,3,2,1,0:T(8,128)(2,1)} fusion(bf16[2048,1024]{1,0:T(8,128)(2,1)} %param.6, bf16[1,4,4,16,1024]{4,3,2,1,0:T(8,128)(2,1)S(1)} %add_convert_fusion), kind=kOutput, calls=%fused_computation.150 | convolution fusion | flops 1074266112 | bytes 5767168 | tf_op jit(solution)/shard_map/dot_general | solution.py:132
  192.9 0.0 reduce-scatter.6.cloned.1.call-update
  192.9 0.0 reduce-scatter.8.cloned.1.call-start
  193.0 4.6 %fusion.9 = bf16[2048,1024]{0,1:T(8,128)(2,1)} fusion(bf16[1,4,4,16,2048]{4,3,2,1,0:T(8,128)(2,1)} %all-gather.2.cloned.1.call-done, f32[1,4,4,16,1024]{4,3,2,1,0:T(8,128)S(1)} %copy-done.9), kind=kOutput, calls=%fused_computation.142 | convolution fusion | flops 1077149696 | bytes 6291456 | tf_op jit(solution)/shard_map/dot_general | solution.py:89
  197.6 3.3 bitcast_convert_fusion.1
  200.9 8.4 %pad_maximum_fusion = bf16[2048,2048]{0,1:T(8,128)(2,1)} fusion(bf16[2048,1024]{0,1:T(8,128)(2,1)} %fusion.9, bf16[2048,1024]{0,1:T(8,128)(2,1)} %bitcast_convert_fusion.1), kind=kLoop, calls=%fused_computation.130 | loop fusion | flops 16777216 | bytes 16777216 | tf_op jit(solution)/shard_map/concatenate | solution.py:139
  209.2 0.0 reduce-scatter.8.cloned.1.call-update
  209.3 0.0 all-reduce.4.cloned.1.call-done
  209.3 1.8 convert_element_type.1202
  211.1 21.1 %reduce-scatter.4.cloned.1.call-done = bf16[1,4,4,16,512]{4,3,2,1,0:T(8,128)(2,1)} async-done(((bf16[1,4,4,16,2048]{4,3,2,1,0:T(8,128)(2,1)}), bf16[1,4,4,16,512]{4,3,2,1,0:T(8,128)(2,1)}) %reduce-scatter.4.cloned.1.call-update) | async-done | bytes 262160 | tf_op jit(solution)/shard_map/reduce_scatter | solution.py:80
  232.2 1.7 add_convert_fusion.2
  234.0 26.2 %reduce-scatter.6.cloned.1.call-done = bf16[1,4,4,16,512]{4,3,2,1,0:T(8,128)(2,1)} async-done(((bf16[1,4,4,16,2048]{4,3,2,1,0:T(8,128)(2,1)}), bf16[1,4,4,16,512]{4,3,2,1,0:T(8,128)(2,1)}) %reduce-scatter.6.cloned.1.call-update) | async-done | bytes 262160 | tf_op jit(solution)/shard_map/reduce_scatter | solution.py:80
  260.2 1.7 add_convert_fusion.1
  261.9 71.9 %reduce-scatter.8.cloned.1.call-done = bf16[256,2048]{0,1:T(8,128)(2,1)} async-done(((bf16[2048,2048]{0,1:T(8,128)(2,1)}), bf16[256,2048]{0,1:T(8,128)(2,1)}) %reduce-scatter.8.cloned.1.call-update) | async-done | bytes 1048592 | tf_op jit(solution)/shard_map/reduce_scatter | solution.py:138
  333.9 1.3 fusion.333
  335.1 1.0 copy.11
  336.1 1.0 copy.10
  (345 shorter events, 1.2 us)
Async XLA Ops:
  7.2 100.7 %all-gather.2.cloned.1.call-start = ((), (), s32[]{:S(2)}) async-start(), calls=%async_computation.4 | async-start | bytes 1310720 | tf_op jit(solution)/shard_map/all_gather | solution.py:101
  7.9 201.4 %all-reduce.4.cloned.1.call-start = ((), (), s32[]{:S(2)}) async-start(), calls=%async_computation.7 | async-start | bytes 524288 | tf_op jit(solution)/shard_map/psum | solution.py:127
  7.9 9.9 %collective-permute-start = (bf16[1,4,4,16,512]{4,3,2,1,0:T(8,128)(2,1)}, bf16[1,4,4,16,512]{4,3,2,1,0:T(8,128)(2,1)S(1)}, u32[]{:S(2)}, u32[]{:S(2)}) collective-permute-start(bf16[1,4,4,16,512]{4,3,2,1,0:T(8,128)(2,1)} %param.5), channel_id=1, source_target_pairs={{0,1},{1,0},{2,3},{3,2},{4,5},{5,4},{6,7},{7,6},{8,9},{9,8},{10,11... | collective-permute-start | bytes 786440 | tf_op jit(solution)/shard_map/ppermute | solution.py:11
  17.6 60.0 %copy-start.54 = (f32[1,1024]{1,0:T(1,128)}, f32[1,1024]{1,0:T(1,128)S(1)}, u32[]{:S(2)}) copy-start(f32[1,1024]{1,0:T(1,128)S(1)} %get-tuple-element.162) | copy-start | bytes 12292
  17.6 60.0 %copy-start.56 = (f32[1,1024]{1,0:T(1,128)}, f32[1,1024]{1,0:T(1,128)S(1)}, u32[]{:S(2)}) copy-start(f32[1,1024]{1,0:T(1,128)S(1)} %get-tuple-element.163) | copy-start | bytes 12292
  17.6 60.0 %copy-start.58 = (f32[1,1024]{1,0:T(1,128)}, f32[1,1024]{1,0:T(1,128)S(1)}, u32[]{:S(2)}) copy-start(f32[1,1024]{1,0:T(1,128)S(1)} %get-tuple-element.164) | copy-start | bytes 12292
  17.7 60.0 %copy-start.60 = (f32[1,1024]{1,0:T(1,128)}, f32[1,1024]{1,0:T(1,128)S(1)}, u32[]{:S(2)}) copy-start(f32[1,1024]{1,0:T(1,128)S(1)} %get-tuple-element.165) | copy-start | bytes 12292
  17.7 60.0 %copy-start.62 = (f32[1,1024]{1,0:T(1,128)}, f32[1,1024]{1,0:T(1,128)S(1)}, u32[]{:S(2)}) copy-start(f32[1,1024]{1,0:T(1,128)S(1)} %get-tuple-element.166) | copy-start | bytes 12292
  17.7 60.0 %copy-start.64 = (f32[1,1024]{1,0:T(1,128)}, f32[1,1024]{1,0:T(1,128)S(1)}, u32[]{:S(2)}) copy-start(f32[1,1024]{1,0:T(1,128)S(1)} %get-tuple-element.167) | copy-start | bytes 12292
  17.7 60.0 %copy-start.66 = (f32[1,1024]{1,0:T(1,128)}, f32[1,1024]{1,0:T(1,128)S(1)}, u32[]{:S(2)}) copy-start(f32[1,1024]{1,0:T(1,128)S(1)} %get-tuple-element.168) | copy-start | bytes 12292
  17.7 60.0 %copy-start.68 = (f32[1,1024]{1,0:T(1,128)}, f32[1,1024]{1,0:T(1,128)S(1)}, u32[]{:S(2)}) copy-start(f32[1,1024]{1,0:T(1,128)S(1)} %get-tuple-element.169) | copy-start | bytes 12292
  17.7 60.0 %copy-start.70 = (f32[1,1024]{1,0:T(1,128)}, f32[1,1024]{1,0:T(1,128)S(1)}, u32[]{:S(2)}) copy-start(f32[1,1024]{1,0:T(1,128)S(1)} %get-tuple-element.170) | copy-start | bytes 12292
  17.7 60.0 %copy-start.72 = (f32[1,1024]{1,0:T(1,128)}, f32[1,1024]{1,0:T(1,128)S(1)}, u32[]{:S(2)}) copy-start(f32[1,1024]{1,0:T(1,128)S(1)} %get-tuple-element.171) | copy-start | bytes 12292
  17.7 60.0 %copy-start.74 = (f32[1,1024]{1,0:T(1,128)}, f32[1,1024]{1,0:T(1,128)S(1)}, u32[]{:S(2)}) copy-start(f32[1,1024]{1,0:T(1,128)S(1)} %get-tuple-element.172) | copy-start | bytes 12292
  17.7 60.0 %copy-start.76 = (f32[1,1024]{1,0:T(1,128)}, f32[1,1024]{1,0:T(1,128)S(1)}, u32[]{:S(2)}) copy-start(f32[1,1024]{1,0:T(1,128)S(1)} %get-tuple-element.173) | copy-start | bytes 12292
  17.7 60.0 %copy-start.78 = (f32[1,1024]{1,0:T(1,128)}, f32[1,1024]{1,0:T(1,128)S(1)}, u32[]{:S(2)}) copy-start(f32[1,1024]{1,0:T(1,128)S(1)} %get-tuple-element.174) | copy-start | bytes 12292
  17.8 60.0 %copy-start.80 = (f32[1,1024]{1,0:T(1,128)}, f32[1,1024]{1,0:T(1,128)S(1)}, u32[]{:S(2)}) copy-start(f32[1,1024]{1,0:T(1,128)S(1)} %get-tuple-element.175) | copy-start | bytes 12292
  17.8 60.0 %copy-start.82 = (f32[1,1024]{1,0:T(1,128)}, f32[1,1024]{1,0:T(1,128)S(1)}, u32[]{:S(2)}) copy-start(f32[1,1024]{1,0:T(1,128)S(1)} %get-tuple-element.176) | copy-start | bytes 12292
  17.8 60.0 %copy-start.84 = (f32[1,1024]{1,0:T(1,128)}, f32[1,1024]{1,0:T(1,128)S(1)}, u32[]{:S(2)}) copy-start(f32[1,1024]{1,0:T(1,128)S(1)} %get-tuple-element.177) | copy-start | bytes 12292
  17.8 60.0 %copy-start.86 = (f32[1,1024]{1,0:T(1,128)}, f32[1,1024]{1,0:T(1,128)S(1)}, u32[]{:S(2)}) copy-start(f32[1,1024]{1,0:T(1,128)S(1)} %get-tuple-element.178) | copy-start | bytes 12292
  17.8 60.0 %copy-start.88 = (f32[1,1024]{1,0:T(1,128)}, f32[1,1024]{1,0:T(1,128)S(1)}, u32[]{:S(2)}) copy-start(f32[1,1024]{1,0:T(1,128)S(1)} %get-tuple-element.179) | copy-start | bytes 12292
  17.8 60.0 %copy-start.90 = (f32[1,1024]{1,0:T(1,128)}, f32[1,1024]{1,0:T(1,128)S(1)}, u32[]{:S(2)}) copy-start(f32[1,1024]{1,0:T(1,128)S(1)} %get-tuple-element.180) | copy-start | bytes 12292
  19.1 42.4 %collective-permute-start.1 = (bf16[1,4,4,16,1024]{4,3,2,1,0:T(8,128)(2,1)S(1)}, bf16[1,4,4,16,1024]{4,3,2,1,0:T(8,128)(2,1)S(1)}, u32[]{:S(2)}, u32[]{:S(2)}) collective-permute-start(bf16[1,4,4,16,1024]{4,3,2,1,0:T(8,128)(2,1)S(1)} %maximum_select_fusion.5), channel_id=1, source_target_pairs={{0,2},{1,3},{2,0},{3,1},{4,6},{5,7},{6,4},{7,5},{8,10},{9,11},{10,... | collective-permute-start | bytes 1572872 | tf_op jit(solution)/shard_map/ppermute | solution.py:11
  23.7 54.0 %copy-start.91 = (f32[1,1024]{1,0:T(1,128)}, f32[1,1024]{1,0:T(1,128)S(1)}, u32[]{:S(2)}) copy-start(f32[1,1024]{1,0:T(1,128)S(1)} %get-tuple-element.143) | copy-start | bytes 12292
  23.7 54.0 %copy-start.92 = (f32[1,1024]{1,0:T(1,128)}, f32[1,1024]{1,0:T(1,128)S(1)}, u32[]{:S(2)}) copy-start(f32[1,1024]{1,0:T(1,128)S(1)} %get-tuple-element.144) | copy-start | bytes 12292
  23.8 54.0 %copy-start.93 = (f32[1,1024]{1,0:T(1,128)}, f32[1,1024]{1,0:T(1,128)S(1)}, u32[]{:S(2)}) copy-start(f32[1,1024]{1,0:T(1,128)S(1)} %get-tuple-element.145) | copy-start | bytes 12292
  23.8 54.0 %copy-start.94 = (f32[1,1024]{1,0:T(1,128)}, f32[1,1024]{1,0:T(1,128)S(1)}, u32[]{:S(2)}) copy-start(f32[1,1024]{1,0:T(1,128)S(1)} %get-tuple-element.146) | copy-start | bytes 12292
  23.8 54.0 %copy-start.95 = (f32[1,1024]{1,0:T(1,128)}, f32[1,1024]{1,0:T(1,128)S(1)}, u32[]{:S(2)}) copy-start(f32[1,1024]{1,0:T(1,128)S(1)} %get-tuple-element.147) | copy-start | bytes 12292
  23.8 54.0 %copy-start.96 = (f32[1,1024]{1,0:T(1,128)}, f32[1,1024]{1,0:T(1,128)S(1)}, u32[]{:S(2)}) copy-start(f32[1,1024]{1,0:T(1,128)S(1)} %get-tuple-element.148) | copy-start | bytes 12292
  23.8 54.0 %copy-start.97 = (f32[1,1024]{1,0:T(1,128)}, f32[1,1024]{1,0:T(1,128)S(1)}, u32[]{:S(2)}) copy-start(f32[1,1024]{1,0:T(1,128)S(1)} %get-tuple-element.149) | copy-start | bytes 12292
  23.8 54.0 %copy-start.98 = (f32[1,1024]{1,0:T(1,128)}, f32[1,1024]{1,0:T(1,128)S(1)}, u32[]{:S(2)}) copy-start(f32[1,1024]{1,0:T(1,128)S(1)} %get-tuple-element.150) | copy-start | bytes 12292
  23.8 54.0 %copy-start.99 = (f32[1,1024]{1,0:T(1,128)}, f32[1,1024]{1,0:T(1,128)S(1)}, u32[]{:S(2)}) copy-start(f32[1,1024]{1,0:T(1,128)S(1)} %get-tuple-element.151) | copy-start | bytes 12292
  23.8 54.0 %copy-start.100 = (f32[1,1024]{1,0:T(1,128)}, f32[1,1024]{1,0:T(1,128)S(1)}, u32[]{:S(2)}) copy-start(f32[1,1024]{1,0:T(1,128)S(1)} %get-tuple-element.152) | copy-start | bytes 12292
  23.8 54.0 %copy-start.101 = (f32[1,1024]{1,0:T(1,128)}, f32[1,1024]{1,0:T(1,128)S(1)}, u32[]{:S(2)}) copy-start(f32[1,1024]{1,0:T(1,128)S(1)} %get-tuple-element.153) | copy-start | bytes 12292
  23.8 54.0 %copy-start.102 = (f32[1,1024]{1,0:T(1,128)}, f32[1,1024]{1,0:T(1,128)S(1)}, u32[]{:S(2)}) copy-start(f32[1,1024]{1,0:T(1,128)S(1)} %get-tuple-element.154) | copy-start | bytes 12292
  23.9 54.0 %copy-start.103 = (f32[1,1024]{1,0:T(1,128)}, f32[1,1024]{1,0:T(1,128)S(1)}, u32[]{:S(2)}) copy-start(f32[1,1024]{1,0:T(1,128)S(1)} %get-tuple-element.155) | copy-start | bytes 12292
  23.9 54.0 %copy-start.104 = (f32[1,1024]{1,0:T(1,128)}, f32[1,1024]{1,0:T(1,128)S(1)}, u32[]{:S(2)}) copy-start(f32[1,1024]{1,0:T(1,128)S(1)} %get-tuple-element.156) | copy-start | bytes 12292
  23.9 54.0 %copy-start.105 = (f32[1,1024]{1,0:T(1,128)}, f32[1,1024]{1,0:T(1,128)S(1)}, u32[]{:S(2)}) copy-start(f32[1,1024]{1,0:T(1,128)S(1)} %get-tuple-element.157) | copy-start | bytes 12292
  23.9 54.0 %copy-start.106 = (f32[1,1024]{1,0:T(1,128)}, f32[1,1024]{1,0:T(1,128)S(1)}, u32[]{:S(2)}) copy-start(f32[1,1024]{1,0:T(1,128)S(1)} %get-tuple-element.158) | copy-start | bytes 12292
  23.9 54.0 %copy-start.107 = (f32[1,1024]{1,0:T(1,128)}, f32[1,1024]{1,0:T(1,128)S(1)}, u32[]{:S(2)}) copy-start(f32[1,1024]{1,0:T(1,128)S(1)} %get-tuple-element.159) | copy-start | bytes 12292
  65.2 12.7 %copy-start.2 = (bf16[256,1024]{1,0:T(8,128)(2,1)}, bf16[256,1024]{1,0:T(8,128)(2,1)S(1)}, u32[]{:S(2)}) copy-start(bf16[256,1024]{1,0:T(8,128)(2,1)S(1)} %convolution_convert_fusion) | copy-start | bytes 1572868
  65.3 12.7 %copy-start.12 = (f32[1,1024]{1,0:T(1,128)S(1)}, f32[1,1024]{1,0:T(1,128)}, u32[]{:S(2)}) copy-start(f32[1,1024]{1,0:T(1,128)} %get-tuple-element.217) | copy-start | bytes 12292
  65.3 12.7 %copy-start.14 = (f32[1,1024]{1,0:T(1,128)S(1)}, f32[1,1024]{1,0:T(1,128)}, u32[]{:S(2)}) copy-start(f32[1,1024]{1,0:T(1,128)} %get-tuple-element.218) | copy-start | bytes 12292
  65.3 12.7 %copy-start.16 = (f32[1,1024]{1,0:T(1,128)S(1)}, f32[1,1024]{1,0:T(1,128)}, u32[]{:S(2)}) copy-start(f32[1,1024]{1,0:T(1,128)} %get-tuple-element.181) | copy-start | bytes 12292
  65.3 12.7 %copy-start.18 = (f32[1,1024]{1,0:T(1,128)S(1)}, f32[1,1024]{1,0:T(1,128)}, u32[]{:S(2)}) copy-start(f32[1,1024]{1,0:T(1,128)} %get-tuple-element.182) | copy-start | bytes 12292
  65.3 12.7 %copy-start.20 = (f32[1,1024]{1,0:T(1,128)S(1)}, f32[1,1024]{1,0:T(1,128)}, u32[]{:S(2)}) copy-start(f32[1,1024]{1,0:T(1,128)} %get-tuple-element.183) | copy-start | bytes 12292
  65.3 12.7 %copy-start.22 = (f32[1,1024]{1,0:T(1,128)S(1)}, f32[1,1024]{1,0:T(1,128)}, u32[]{:S(2)}) copy-start(f32[1,1024]{1,0:T(1,128)} %get-tuple-element.184) | copy-start | bytes 12292
  65.3 12.7 %copy-start.24 = (f32[1,1024]{1,0:T(1,128)S(1)}, f32[1,1024]{1,0:T(1,128)}, u32[]{:S(2)}) copy-start(f32[1,1024]{1,0:T(1,128)} %get-tuple-element.185) | copy-start | bytes 12292
  65.3 12.7 %copy-start.26 = (f32[1,1024]{1,0:T(1,128)S(1)}, f32[1,1024]{1,0:T(1,128)}, u32[]{:S(2)}) copy-start(f32[1,1024]{1,0:T(1,128)} %get-tuple-element.186) | copy-start | bytes 12292
  65.3 12.7 %copy-start.28 = (f32[1,1024]{1,0:T(1,128)S(1)}, f32[1,1024]{1,0:T(1,128)}, u32[]{:S(2)}) copy-start(f32[1,1024]{1,0:T(1,128)} %get-tuple-element.187) | copy-start | bytes 12292
  65.4 12.7 %copy-start.30 = (f32[1,1024]{1,0:T(1,128)S(1)}, f32[1,1024]{1,0:T(1,128)}, u32[]{:S(2)}) copy-start(f32[1,1024]{1,0:T(1,128)} %get-tuple-element.188) | copy-start | bytes 12292
  65.4 12.7 %copy-start.32 = (f32[1,1024]{1,0:T(1,128)S(1)}, f32[1,1024]{1,0:T(1,128)}, u32[]{:S(2)}) copy-start(f32[1,1024]{1,0:T(1,128)} %get-tuple-element.189) | copy-start | bytes 12292
  65.4 12.7 %copy-start.34 = (f32[1,1024]{1,0:T(1,128)S(1)}, f32[1,1024]{1,0:T(1,128)}, u32[]{:S(2)}) copy-start(f32[1,1024]{1,0:T(1,128)} %get-tuple-element.190) | copy-start | bytes 12292
  65.4 12.7 %copy-start.36 = (f32[1,1024]{1,0:T(1,128)S(1)}, f32[1,1024]{1,0:T(1,128)}, u32[]{:S(2)}) copy-start(f32[1,1024]{1,0:T(1,128)} %get-tuple-element.191) | copy-start | bytes 12292
  65.5 11.2 %collective-permute-start.3 = (bf16[1,2,4,16,1024]{4,3,2,1,0:T(8,128)(2,1)S(1)}, bf16[1,2,4,16,1024]{4,3,2,1,0:T(8,128)(2,1)S(1)}, u32[]{:S(2)}, u32[]{:S(2)}) collective-permute-start(bf16[1,2,4,16,1024]{4,3,2,1,0:T(8,128)(2,1)S(1)} %get-tuple-element.141), channel_id=1, source_target_pairs={{4,0},{8,4},{12,8},{5,1},{9,5},{13,9},{6,2},{10,6},{14,10},{7,3},{... | collective-permute-start | bytes 786440 | tf_op jit(solution)/shard_map/ppermute | solution.py:27
  66.9 9.8 %collective-permute-start.2 = (bf16[1,2,4,16,1024]{4,3,2,1,0:T(8,128)(2,1)S(1)}, bf16[1,2,4,16,1024]{4,3,2,1,0:T(8,128)(2,1)S(1)}, u32[]{:S(2)}, u32[]{:S(2)}) collective-permute-start(bf16[1,2,4,16,1024]{4,3,2,1,0:T(8,128)(2,1)S(1)} %get-tuple-element.142), channel_id=1, source_target_pairs={{0,4},{4,8},{8,12},{1,5},{5,9},{9,13},{2,6},{6,10},{10,14},{3,7},{... | collective-permute-start | bytes 786440 | tf_op jit(solution)/shard_map/ppermute | solution.py:26
  114.2 16.9 %copy-start = (bf16[1,4,4,16,1024]{4,3,2,1,0:T(8,128)(2,1)}, bf16[1,4,4,16,1024]{4,3,2,1,0:T(8,128)(2,1)S(1)}, u32[]{:S(2)}) copy-start(bf16[1,4,4,16,1024]{4,3,2,1,0:T(8,128)(2,1)S(1)} %get-tuple-element.268) | copy-start | bytes 1572868
  131.0 20.7 %copy-start.9 = (f32[1,4,4,16,1024]{4,3,2,1,0:T(8,128)S(1)}, f32[1,4,4,16,1024]{4,3,2,1,0:T(8,128)}, u32[]{:S(2)}) copy-start(f32[1,4,4,16,1024]{4,3,2,1,0:T(8,128)} %fusion.158) | copy-start | bytes 3145732
  143.8 88.4 %reduce-scatter.4.cloned.1.call-start = ((), (), s32[]{:S(2)}) async-start(), calls=%async_computation.3 | async-start | bytes 1310720 | tf_op jit(solution)/shard_map/reduce_scatter | solution.py:80
  143.9 12.7 %collective-permute-start.5 = (bf16[1,2,4,16,1024]{4,3,2,1,0:T(8,128)(2,1)S(1)}, bf16[1,2,4,16,1024]{4,3,2,1,0:T(8,128)(2,1)S(1)}, u32[]{:S(2)}, u32[]{:S(2)}) collective-permute-start(bf16[1,2,4,16,1024]{4,3,2,1,0:T(8,128)(2,1)S(1)} %get-tuple-element.139), channel_id=1, source_target_pairs={{4,0},{8,4},{12,8},{5,1},{9,5},{13,9},{6,2},{10,6},{14,10},{7,3},{... | collective-permute-start | bytes 786440 | tf_op jit(solution)/shard_map/ppermute | solution.py:27
  145.2 11.4 %collective-permute-start.4 = (bf16[1,2,4,16,1024]{4,3,2,1,0:T(8,128)(2,1)S(1)}, bf16[1,2,4,16,1024]{4,3,2,1,0:T(8,128)(2,1)S(1)}, u32[]{:S(2)}, u32[]{:S(2)}) collective-permute-start(bf16[1,2,4,16,1024]{4,3,2,1,0:T(8,128)(2,1)S(1)} %get-tuple-element.140), channel_id=1, source_target_pairs={{0,4},{4,8},{8,12},{1,5},{5,9},{9,13},{2,6},{6,10},{10,14},{3,7},{... | collective-permute-start | bytes 786440 | tf_op jit(solution)/shard_map/ppermute | solution.py:26
  156.5 103.7 %reduce-scatter.6.cloned.1.call-start = ((), (), s32[]{:S(2)}) async-start(), calls=%async_computation.5 | async-start | bytes 1310720 | tf_op jit(solution)/shard_map/reduce_scatter | solution.py:80
  192.9 140.9 %reduce-scatter.8.cloned.1.call-start = ((), (), s32[]{:S(2)}) async-start(), calls=%async_computation.6 | async-start | bytes 9437184 | tf_op jit(solution)/shard_map/reduce_scatter | solution.py:138
  209.2 51.0 %copy-start.10 = (bf16[1,4,4,16,512]{4,3,2,1,0:T(8,128)(2,1)S(1)}, bf16[1,4,4,16,512]{4,3,2,1,0:T(8,128)(2,1)}, u32[]{:S(2)}) copy-start(bf16[1,4,4,16,512]{4,3,2,1,0:T(8,128)(2,1)} %param.9) | copy-start | bytes 786436
  (57 other events, 212.3 us)
Sparse Core Ops, SparseCore 0:
  9.6 49.9 all-gather.1
  143.9 59.2 all-reduce.3
  205.6 26.5 reduce-scatter.3
  234.4 25.7 reduce-scatter.5
  263.9 69.9 reduce-scatter.7
